TPU v7x, 32 devices: a whole 2x2x4 slice. The times are simulated.
32 devices in a mesh: emit: 4 (over z), elem: 8 (over y, x, core).
Axes of the slice: x: 2, y: 2, z: 4, core: 2. Of those that a mesh axis runs over, the one named last changes fastest.
Arguments:
- traces: float32 [256, 1024, 1024], P('emit', 'elem'), may hold values from -6 to 6
- codes: float32 [4, 2, 128], replicated, may hold values from -0.5 to 0.5
- code_of: int32 [256], replicated, may hold values from 0 to 3
- order: int32 [256], replicated, may hold values from 0 to 255, each once
- steer: float32 [256, 1024, 256], P(None, 'elem'), may hold values from -0.1875 to 0.1875
Outputs:
- beams: float32 [256, 256, 256], P('elem', 'emit')
Inputs may be any that keep to these rules, and one draw needn't show every extreme that they name: `order`: each value 0 to 255 appears exactly once.
All inputs are finite; a program needn't handle non-finite values.
Results may differ from a plain program's by a relative error of at most 0.000071.
Values sent between devices are 32-bit elements; how exact they have to be, the bound alone decides.
No kernel may reach another device: no remote copies, remote signals or barrier semaphores. Data moves between devices by JAX's collectives and lax.ppermute only.
A program may use at most 320 MiB of HBM per device.

v0:
```python
import jax
import jax.numpy as jnp
from jax import lax
from jax.sharding import PartitionSpec as P


def toeplitz_table(codes):
    taps = codes.shape[2]
    rows = jnp.arange(2 * taps, dtype=jnp.int32)[:, None]
    cols = jnp.arange(taps, dtype=jnp.int32)[None, :]
    offset = rows - cols
    inside = (offset >= 0) & (offset < taps)
    clipped = jnp.clip(offset, 0, taps - 1)
    in_phase = jnp.where(inside[None], codes[:, 0, :][:, clipped], 0.0)
    quadrature = jnp.where(inside[None], codes[:, 1, :][:, clipped], 0.0)
    return jnp.concatenate([in_phase, quadrature], axis=2)


def hadamard_signs(order, columns, emissions):
    parity = jnp.zeros((order.shape[0], columns.shape[0]), jnp.int32)
    for bit in range(emissions.bit_length()):
        parity = parity + (order[:, None] >> bit & columns[None, :] >> bit & 1)
    signs = (1 - 2 * (parity % 2)).astype(jnp.float32)
    return signs / jnp.sqrt(jnp.float32(emissions))


def spectral_table(samples, taps, bins):
    rows = jnp.arange(samples // taps * 2 * taps, dtype=jnp.int32)
    block = rows // (2 * taps)
    quad = rows // taps % 2
    sample = block * taps + rows % taps
    freqs = jnp.arange(bins, dtype=jnp.int32) - bins // 2
    phase = jnp.mod(sample[:, None] * freqs[None, :], samples).astype(jnp.float32)
    angle = phase * (2.0 * jnp.pi / samples)
    cosine = jnp.cos(angle)
    sine = jnp.sin(angle)
    is_quad = quad[:, None] == 1
    real_cols = jnp.where(is_quad, sine, cosine)
    imag_cols = jnp.where(is_quad, cosine, -sine)
    return jnp.concatenate([real_cols, imag_cols], axis=1) / jnp.sqrt(jnp.float32(samples))


def steer_bins(source, steer, count, contract):
    bins = steer.shape[0]
    half = steer.shape[2] // 2
    real_part = lax.slice_in_dim(source, 0, count, axis=0)
    imag_part = lax.dynamic_slice_in_dim(source, bins, count, 0)
    numbers = (((contract,), (1,)), ((0,), (0,)))
    first = lax.dot_general(real_part, steer, numbers, precision=lax.Precision.HIGHEST)
    second = lax.dot_general(imag_part, steer, numbers, precision=lax.Precision.HIGHEST)
    return jnp.concatenate(
        [first[..., :half] - second[..., half:], first[..., half:] + second[..., :half]], axis=2
    )


def per_device(traces, codes, code_of, order, steer):
    edev, mdev, samples = traces.shape
    ncode, taps = (codes.shape[0], codes.shape[2])
    emissions = order.shape[0]
    bins = steer.shape[0]
    bins_dev = bins // lax.axis_size("elem")
    nblock = samples // taps
    first = lax.axis_index("emit") * edev
    own_codes = lax.dynamic_slice_in_dim(code_of, first, edev)
    onehot = (own_codes[:, None] == jnp.arange(ncode, dtype=jnp.int32)[None, :]).astype(jnp.float32)
    table = toeplitz_table(codes)
    picked = jnp.einsum("ec,cjd->ejd", onehot, table, precision=lax.Precision.HIGHEST)
    blocks = traces.reshape(edev, mdev, nblock, taps)
    current = jnp.einsum(
        "emnj,ejd->emnd", blocks, picked[:, :taps, :], precision=lax.Precision.HIGHEST
    )
    following = jnp.einsum(
        "emnj,ejd->emnd", blocks, picked[:, taps:, :], precision=lax.Precision.HIGHEST
    )
    following = jnp.concatenate(
        [following[:, :, 1:], jnp.zeros((edev, mdev, 1, 2 * taps), jnp.float32)], axis=2
    )
    corr = (current + following).reshape(edev, mdev, nblock * 2 * taps)
    transform = spectral_table(samples, taps, bins)
    spectra = lax.dot_general(
        transform, corr, (((0,), (2,)), ((), ())), precision=lax.Precision.HIGHEST
    )
    columns = first + jnp.arange(edev, dtype=jnp.int32)
    hadamard = hadamard_signs(order, columns, emissions)
    coded = lax.psum_scatter(
        steer_bins(spectra, steer, bins_dev * lax.axis_size("elem"), 2),
        "elem",
        scatter_dimension=0,
        tiled=True,
    )
    folded = lax.dot_general(
        lax.all_gather(coded, "emit", axis=1, tiled=True),
        hadamard,
        (((1,), (0,)), ((), ())),
        precision=lax.Precision.HIGHEST,
    )
    beams = jnp.transpose(folded, (0, 2, 1))
    return beams


def solution(mesh):
    placed = (P("emit", "elem", None), P(), P(), P(), P(None, "elem", None))
    return jax.shard_map(
        per_device, mesh=mesh, in_specs=placed, out_specs=P("elem", "emit", None), check_vma=False
    )
```

profile of v0, /device:TPU:0, one launch (start us, length us, event | category | flops | bytes accessed | tf_op | source)
XLA Modules:
  0.0 971.7 jit_solution(796748638702718246)
XLA Ops:
  6.7 0.8 fusion.103
  7.5 0.1 copy.39
  7.6 109.0 %gather_fusion = f32[32768,4]{1,0:T(8,128)} fusion(f32[4,128]{0,1:T(8,128)S(1)} %bitcast.66, s32[32768]{0:T(1024)S(1)} %fusion.34), kind=kCustom, calls=%fused_computation | custom fusion | bytes 1179648 | tf_op jit(solution)/shard_map/gather | solution.py:14
  116.5 9.4 copy.17
  126.0 0.1 copy.40
  126.1 109.0 %gather_fusion.1 = f32[32768,4]{1,0:T(8,128)} fusion(f32[4,128]{0,1:T(8,128)S(1)} %bitcast.65, s32[32768]{0:T(1024)S(1)} %fusion.34), kind=kCustom, calls=%fused_computation.1 | custom fusion | bytes 1179648 | tf_op jit(solution)/shard_map/gather | solution.py:15
  235.0 9.4 copy.20
  244.6 0.3 select_bitcast_fusion.1
  244.9 7.0 fusion.26
  251.9 6.4 slice_bitcast_fusion.1
  258.3 65.5 %fusion.8 = f32[64,128,8,256]{1,3,2,0:T(8,128)} fusion(f32[64,128,256,1]{2,0,1,3:T(8,128)} %get-tuple-element.10, f32[64,128,1024]{2,1,0:T(8,128)} %param.5), kind=kOutput, calls=%fused_computation.9 | convolution fusion | flops 25769803776 | bytes 109051904 | tf_op jit(solution)/shard_map/emnj,ejd->emnd/dot_general | solution.py:72
  323.8 38.4 %slice.46 = f32[64,128,7,256]{1,3,2,0:T(8,128)} slice(f32[64,128,8,256]{1,3,2,0:T(8,128)} %fusion.8), slice={[0:64], [0:128], [1:8], [0:256]} | slice | bytes 117440512 | tf_op jit(solution)/shard_map/slice | solution.py:76
  362.2 88.9 %bitcast_add_fusion = f32[64,128,8,256]{1,3,2,0:T(8,128)} fusion(f32[64,128,7,256]{1,3,2,0:T(8,128)} %slice.46, f32[64,128,256,1]{2,0,1,3:T(8,128)} %get-tuple-element.9, f32[64,128,1024]{2,1,0:T(8,128)} %param.5), kind=kOutput, calls=%fused_computation.2 | convolution fusion | flops 25786580992 | bytes 167772160 | tf_op jit(solution)/shard_map/emnj,ejd->emnd/dot_general | solution.py:69
  451.1 8.4 fusion.32
  459.5 113.8 %fusion.18 = f32[512,64,128]{2,0,1:T(8,128)} fusion(f32[64,128,2048]{1,2,0:T(8,128)} %bitcast.13, f32[2048,256]{0,1:T(8,128)S(1)} %get-tuple-element.14, f32[2048,256]{0,1:T(8,128)S(1)} %get-tuple-element.13), kind=kOutput, calls=%fused_computation.23 | convolution fusion | flops 103081312256 | bytes 88080384 | tf_op jit(solution)/shard_map/dot_general | solution.py:80
  573.3 11.1 %fusion.102 = (f32[256,64,128]{2,0,1:T(8,128)}, f32[256,64,128]{2,0,1:T(8,128)}) fusion(f32[512,64,128]{2,0,1:T(8,128)} %fusion.18), kind=kLoop, calls=%fused_computation.140 | loop fusion | bytes 33554432 | tf_op jit(solution)/shard_map/slice | solution.py:46
  584.4 34.5 %fusion.13 = f32[256,64,256]{2,1,0:T(8,128)} fusion(f32[256,128,256]{2,1,0:T(8,128)} %param.9, f32[256,64,128]{2,0,1:T(8,128)} %get-tuple-element.8), kind=kOutput, calls=%fused_computation.17 | convolution fusion | flops 6442450944 | bytes 58720256 | tf_op jit(solution)/shard_map/dot_general | solution.py:50
  618.9 34.9 %fusion.15 = f32[256,64,256]{2,1,0:T(8,128)} fusion(f32[256,128,256]{2,1,0:T(8,128)} %param.9, f32[256,64,128]{2,0,1:T(8,128)} %get-tuple-element.7), kind=kOutput, calls=%fused_computation.19 | convolution fusion | flops 6442450944 | bytes 58720256 | tf_op jit(solution)/shard_map/dot_general | solution.py:49
  653.9 18.7 %slice_subtract_fusion = (f32[256,64,128]{2,1,0:T(8,128)}, f32[256,64,128]{2,1,0:T(8,128)}) fusion(f32[256,64,256]{2,1,0:T(8,128)} %fusion.13, f32[256,64,256]{2,1,0:T(8,128)} %fusion.15), kind=kLoop, calls=%fused_computation.12 | loop fusion | flops 4194304 | bytes 50331648 | tf_op jit(solution)/shard_map/sub | solution.py:52
  672.6 11.5 %pad_maximum_fusion = f32[256,64,256]{2,1,0:T(8,128)} fusion(f32[256,64,128]{2,1,0:T(8,128)} %get-tuple-element.6, f32[256,64,128]{2,1,0:T(8,128)} %get-tuple-element.5), kind=kLoop, calls=%fused_computation.10 | loop fusion | flops 4194304 | bytes 33554432 | tf_op jit(solution)/shard_map/concatenate | solution.py:51
  684.1 0.2 all-gather.2.cloned.1.call-start
  684.3 118.8 %reduce-scatter.2.cloned.1.call-done = f32[32,64,256]{2,1,0:T(8,128)} async-done(((f32[256,64,256]{2,1,0:T(8,128)}), f32[32,64,256]{2,1,0:T(8,128)}) %reduce-scatter.2.cloned.1.call-update) | async-done | bytes 2097168 | tf_op jit(solution)/shard_map/reduce_scatter | solution.py:85
  803.3 151.1 %all-gather.2.cloned.1.call-done = f32[32,256,256]{2,1,0:T(8,128)} async-done(((f32[32,64,256]{2,1,0:T(8,128)}), f32[32,256,256]{2,1,0:T(8,128)}) %all-gather.2.cloned.1.call-update) | async-done | bytes 8388624 | tf_op jit(solution)/shard_map/all_gather | solution.py:92
  954.4 10.3 %convolution_bitcast_fusion = f32[32,64,256]{2,1,0:T(8,128)} fusion(f32[32,256,256]{2,1,0:T(8,128)} %all-gather.2.cloned.1.call-done, s32[64]{0:T(128)S(1)} %get-tuple-element.26, s32[256]{0:T(256)S(1)} %get-tuple-element.24, s32[64]{0:T(128)S(1)} %get-tuple-element.27, s32[256]{0:T(256)S(1)} %get-tuple-element.25, s32[64]{0:T(128)S(1)} %get-tuple-element.28, ...), kind=kOutput, calls=%fused_computation.36 | convolution fusion | flops 1611284480 | bytes 10497280 | tf_op jit(solution)/shard_map/dot_general | solution.py:91
  (19 shorter events, 0.3 us)
Async XLA Ops:
  6.5 796.6 %reduce-scatter.2.cloned.1.call-start = ((), (), s32[]{:S(2)}) async-start(), calls=%async_computation.1 | async-start | bytes 18874368 | tf_op jit(solution)/shard_map/reduce_scatter | solution.py:85
  235.0 9.4 copy-start.1
  684.1 119.2 %copy-start = (s32[256]{0:T(256)S(1)}, s32[256]{0:T(256)}, u32[]{:S(2)}) copy-start(s32[256]{0:T(256)} %param.8) | copy-start | bytes 3076
  684.1 270.3 %all-gather.2.cloned.1.call-start = ((), (), s32[]{:S(2)}) async-start(), calls=%async_computation.2 | async-start | bytes 10485760 | tf_op jit(solution)/shard_map/all_gather | solution.py:92
Sparse Core Ops, SparseCore 0:
  684.2 118.8 reduce-scatter.1
  804.7 149.6 all-gather.1
where the time goes:
time: 979 us; the launch traced here: 972 us
  matrix products  355 us (36%)
  local copies, waits for them, and re-layouts  294 us (30%)
  waiting for transfers between devices  270 us (28%)
  other arithmetic  39.1 us (4%)
  between operations  13.7 us (1%)
    all_gather x1, waiting for transfers between devices, per_device(): lax.all_gather(coded, 'emit', axis=1, tiled=True)  151 us
    reduce_scatter x1, waiting for transfers between devices, per_device(): lax.psum_scatter(steer_bins(spectra, steer, bins_dev * lax.axis_size('ele...  119 us
    gather x2, local copies, waits for them, and re-layouts, toeplitz_table(): quadrature = jnp.where(inside[None], codes[:, 1, :][:, clipped], 0.0)  118 us
    gather x2, local copies, waits for them, and re-layouts, toeplitz_table(): in_phase = jnp.where(inside[None], codes[:, 0, :][:, clipped], 0.0)  118 us
    dot_general x1, matrix products, per_device(): lax.dot_general(transform, corr, (((0,), (2,)), ((), ())), precision=lax....  114 us
    dot_general x1, matrix products, per_device(): jnp.einsum('emnj,ejd->emnd', blocks, picked[:, :taps, :], precision=lax.P...  88.9 us
    dot_general x1, matrix products, per_device(): jnp.einsum('emnj,ejd->emnd', blocks, picked[:, taps:, :], precision=lax.P...  65.5 us
    slice x1, local copies, waits for them, and re-layouts, per_device(): following[:, :, 1:]  38.4 us
  transfers between devices with their start and end apart: 2, of which 2 were waited for; matrix products, arithmetic and copies ran while one was open for 0% of the time, Pallas kernels for 0%

commit v1 on v0

--- a/solution.py
+++ b/solution.py
@@ -2,6 +2,28 @@
 import jax.numpy as jnp
 from jax import lax
 from jax.sharding import PartitionSpec as P
+
+
+def in_order(blocks, dim):
+    blocks = jnp.moveaxis(blocks, 0, dim)
+    dims = blocks.shape
+    return blocks.reshape(*dims[:dim], dims[dim] * dims[dim + 1], *dims[dim + 2 :])
+
+
+def grow_blocks(x, axis):
+    size = lax.axis_size(axis)
+    pieces = x[None]
+    for level in range(size.bit_length() - 1):
+        apart = 1 << level
+        other = lax.ppermute(pieces, axis, [(i, i ^ apart) for i in range(size)])
+        both = jnp.stack([pieces, other])
+        upper = lax.axis_index(axis) >> level & 1
+        pieces = jnp.where(upper == 0, both, both[::-1]).reshape(-1, *x.shape)
+    return pieces
+
+
+def doubled_up(array, axis, dim):
+    return in_order(grow_blocks(array, axis), dim)
 
 
 def toeplitz_table(codes):
@@ -89,7 +111,7 @@
         tiled=True,
     )
     folded = lax.dot_general(
-        lax.all_gather(coded, "emit", axis=1, tiled=True),
+        doubled_up(coded, "emit", 1),
         hadamard,
         (((1,), (0,)), ((), ())),
         precision=lax.Precision.HIGHEST,

time: 979 us -> 1070 us (1.093)
  waiting for transfers between devices: 270 us -> 345 us
  other arithmetic: 39.1 us -> 51.5 us
    ppermute x0 -> x2, waiting for transfers between devices: none -> 226 us  [grow_blocks(): other = lax.ppermute(pieces, axis, [(i, i ^ apart) for i in range(size)])]
    all_gather x1 -> x0, waiting for transfers between devices: 151 us -> none  [per_device(): lax.all_gather(coded, 'emit', axis=1, tiled=True)]
  transfers between devices with their start and end apart: 2 -> 3, of which waited for: 2 -> 3; matrix products, arithmetic and copies ran while one was open for 0% -> 0% of each run, Pallas kernels for 0% -> 0%
where the time goes in v1:
time: 1070 us; the launch traced here: 1060 us
  matrix products  352 us (33%)
  waiting for transfers between devices  345 us (32%)
  local copies, waits for them, and re-layouts  295 us (28%)
  other arithmetic  51.5 us (5%)
  between operations  13.8 us (1%)
    ppermute x2, waiting for transfers between devices, grow_blocks(): other = lax.ppermute(pieces, axis, [(i, i ^ apart) for i in range(size)])  226 us
    reduce_scatter x1, waiting for transfers between devices, per_device(): lax.psum_scatter(steer_bins(spectra, steer, bins_dev * lax.axis_size('ele...  119 us
    gather x2, local copies, waits for them, and re-layouts, toeplitz_table(): quadrature = jnp.where(inside[None], codes[:, 1, :][:, clipped], 0.0)  118 us
    gather x2, local copies, waits for them, and re-layouts, toeplitz_table(): in_phase = jnp.where(inside[None], codes[:, 0, :][:, clipped], 0.0)  118 us
    dot_general x1, matrix products, per_device(): lax.dot_general(transform, corr, (((0,), (2,)), ((), ())), precision=lax....  114 us
    dot_general x1, matrix products, per_device(): jnp.einsum('emnj,ejd->emnd', blocks, picked[:, :taps, :], precision=lax.P...  88.9 us
    dot_general x1, matrix products, per_device(): jnp.einsum('emnj,ejd->emnd', blocks, picked[:, taps:, :], precision=lax.P...  65.5 us
    slice x1, local copies, waits for them, and re-layouts, per_device(): following[:, :, 1:]  38.4 us
  transfers between devices with their start and end apart: 3, of which 3 were waited for; matrix products, arithmetic and copies ran while one was open for 0% of the time, Pallas kernels for 0%

profile of v1, /device:TPU:0, one launch (start us, length us, event | category | flops | bytes accessed | tf_op | source)
XLA Modules:
  0.0 1060.5 jit_solution(1244423147068834479)
XLA Ops:
  7.6 109.0 %gather_fusion = f32[32768,4]{1,0:T(8,128)} fusion(f32[4,128]{0,1:T(8,128)S(1)} %bitcast.78, s32[32768]{0:T(1024)S(1)} %fusion.36), kind=kCustom, calls=%fused_computation | custom fusion | bytes 1179648 | tf_op jit(solution)/shard_map/gather | solution.py:36
  116.5 9.4 copy.18
  126.1 109.0 %gather_fusion.1 = f32[32768,4]{1,0:T(8,128)} fusion(f32[4,128]{0,1:T(8,128)S(1)} %bitcast.77, s32[32768]{0:T(1024)S(1)} %fusion.36), kind=kCustom, calls=%fused_computation.1 | custom fusion | bytes 1179648 | tf_op jit(solution)/shard_map/gather | solution.py:37
  235.0 9.4 copy.21
  244.9 7.0 fusion.28
  251.9 6.4 slice_bitcast_fusion.1
  258.3 65.5 %fusion.8 = f32[64,128,8,256]{1,3,2,0:T(8,128)} fusion(f32[64,128,256,1]{2,0,1,3:T(8,128)} %get-tuple-element.10, f32[64,128,1024]{2,1,0:T(8,128)} %param.5), kind=kOutput, calls=%fused_computation.9 | convolution fusion | flops 25769803776 | bytes 109051904 | tf_op jit(solution)/shard_map/emnj,ejd->emnd/dot_general | solution.py:94
  323.8 38.4 %slice.46 = f32[64,128,7,256]{1,3,2,0:T(8,128)} slice(f32[64,128,8,256]{1,3,2,0:T(8,128)} %fusion.8), slice={[0:64], [0:128], [1:8], [0:256]} | slice | bytes 117440512 | tf_op jit(solution)/shard_map/slice | solution.py:98
  362.2 88.9 %bitcast_add_fusion = f32[64,128,8,256]{1,3,2,0:T(8,128)} fusion(f32[64,128,7,256]{1,3,2,0:T(8,128)} %slice.46, f32[64,128,256,1]{2,0,1,3:T(8,128)} %get-tuple-element.9, f32[64,128,1024]{2,1,0:T(8,128)} %param.5), kind=kOutput, calls=%fused_computation.2 | convolution fusion | flops 25786580992 | bytes 167772160 | tf_op jit(solution)/shard_map/emnj,ejd->emnd/dot_general | solution.py:91
  451.1 8.4 fusion.34
  459.5 113.8 %fusion.18 = f32[512,64,128]{2,0,1:T(8,128)} fusion(f32[64,128,2048]{1,2,0:T(8,128)} %bitcast.13, f32[2048,256]{0,1:T(8,128)S(1)} %get-tuple-element.16, f32[2048,256]{0,1:T(8,128)S(1)} %get-tuple-element.15), kind=kOutput, calls=%fused_computation.26 | convolution fusion | flops 103081312256 | bytes 88080384 | tf_op jit(solution)/shard_map/dot_general | solution.py:102
  573.3 11.1 %fusion.104 = (f32[256,64,128]{2,0,1:T(8,128)}, f32[256,64,128]{2,0,1:T(8,128)}) fusion(f32[512,64,128]{2,0,1:T(8,128)} %fusion.18), kind=kLoop, calls=%fused_computation.146 | loop fusion | bytes 33554432 | tf_op jit(solution)/shard_map/slice | solution.py:68
  584.4 34.5 %fusion.13 = f32[256,64,256]{2,1,0:T(8,128)} fusion(f32[256,128,256]{2,1,0:T(8,128)} %param.9, f32[256,64,128]{2,0,1:T(8,128)} %get-tuple-element.8), kind=kOutput, calls=%fused_computation.19 | convolution fusion | flops 6442450944 | bytes 58720256 | tf_op jit(solution)/shard_map/dot_general | solution.py:72
  618.9 34.9 %fusion.15 = f32[256,64,256]{2,1,0:T(8,128)} fusion(f32[256,128,256]{2,1,0:T(8,128)} %param.9, f32[256,64,128]{2,0,1:T(8,128)} %get-tuple-element.7), kind=kOutput, calls=%fused_computation.21 | convolution fusion | flops 6442450944 | bytes 58720256 | tf_op jit(solution)/shard_map/dot_general | solution.py:71
  653.9 18.7 %slice_subtract_fusion = (f32[256,64,128]{2,1,0:T(8,128)}, f32[256,64,128]{2,1,0:T(8,128)}) fusion(f32[256,64,256]{2,1,0:T(8,128)} %fusion.13, f32[256,64,256]{2,1,0:T(8,128)} %fusion.15), kind=kLoop, calls=%fused_computation.13 | loop fusion | flops 4194304 | bytes 50331648 | tf_op jit(solution)/shard_map/sub | solution.py:74
  672.6 11.7 %pad_maximum_fusion = f32[256,64,256]{2,1,0:T(8,128)} fusion(f32[256,64,128]{2,1,0:T(8,128)} %get-tuple-element.6, f32[256,64,128]{2,1,0:T(8,128)} %get-tuple-element.5), kind=kLoop, calls=%fused_computation.10 | loop fusion | flops 4194304 | bytes 33554432 | tf_op jit(solution)/shard_map/concatenate | solution.py:73
  684.3 119.0 %reduce-scatter.2.cloned.1.call-done = f32[32,64,256]{2,1,0:T(8,128)} async-done(((f32[256,64,256]{2,1,0:T(8,128)}), f32[32,64,256]{2,1,0:T(8,128)}) %reduce-scatter.2.cloned.1.call-update) | async-done | bytes 2097168 | tf_op jit(solution)/shard_map/reduce_scatter | solution.py:107
  804.8 45.9 %collective-permute-done = f32[1,32,64,256]{3,2,1,0:T(8,128)S(1)} collective-permute-done((f32[1,32,64,256]{3,2,1,0:T(8,128)}, f32[1,32,64,256]{3,2,1,0:T(8,128)S(1)}, u32[]{:S(2)}, u32[]{:S(2)}) %collective-permute-start) | collective-permute-done | bytes 2097184 | tf_op jit(solution)/shard_map/ppermute | solution.py:18
  850.7 2.0 pad_maximum_fusion.2
  852.7 4.6 fusion.23
  857.3 2.4 collective-permute-start.1
  859.8 179.9 %collective-permute-done.1 = f32[2,32,64,256]{3,2,1,0:T(8,128)} collective-permute-done((f32[2,32,64,256]{3,2,1,0:T(8,128)}, f32[2,32,64,256]{3,2,1,0:T(8,128)}, u32[]{:S(2)}, u32[]{:S(2)}) %collective-permute-start.1) | collective-permute-done | bytes 4194336 | tf_op jit(solution)/shard_map/ppermute | solution.py:18
  1039.7 4.1 pad_maximum_fusion.1
  1046.6 6.9 convolution_bitcast_fusion
  (25 shorter events, 5.8 us)
Async XLA Ops:
  6.5 796.8 %reduce-scatter.2.cloned.1.call-start = ((), (), s32[]{:S(2)}) async-start(), calls=%async_computation.1 | async-start | bytes 18874368 | tf_op jit(solution)/shard_map/reduce_scatter | solution.py:107
  235.0 9.4 copy-start.1
  803.3 47.4 %collective-permute-start = (f32[1,32,64,256]{3,2,1,0:T(8,128)}, f32[1,32,64,256]{3,2,1,0:T(8,128)S(1)}, u32[]{:S(2)}, u32[]{:S(2)}) collective-permute-start(f32[1,32,64,256]{3,2,1,0:T(8,128)} %bitcast.83), channel_id=1, source_target_pairs={{0,8},{8,0},{16,24},{24,16},{1,9},{9,1},{17,25},{25,17},{2,10},{10... | collective-permute-start | bytes 6291464 | tf_op jit(solution)/shard_map/ppermute | solution.py:18
  852.7 7.0 copy-start
  857.3 182.4 %collective-permute-start.1 = (f32[2,32,64,256]{3,2,1,0:T(8,128)}, f32[2,32,64,256]{3,2,1,0:T(8,128)}, u32[]{:S(2)}, u32[]{:S(2)}) collective-permute-start(f32[2,32,64,256]{3,2,1,0:T(8,128)} %get-tuple-element.12), channel_id=1, source_target_pairs={{0,16},{8,24},{16,0},{24,8},{1,17},{9,25},{17,1},{25,9},{2,18},{10... | collective-permute-start | bytes 12582920 | tf_op jit(solution)/shard_map/ppermute | solution.py:18
Sparse Core Ops, SparseCore 0:
  684.4 118.8 reduce-scatter.1
